TPU v7x, 512 devices: a whole 4x8x8 slice. The times are simulated.
512 devices in a mesh: dp: 4 (over x_hi, core), context: 16 (over x_lo, z), tensor: 8 (over y).
Axes of the slice: x: 4 (x_hi: 2, x_lo: 2; x = x_hi * 2 + x_lo), y: 8, z: 8, core: 2. Of those that a mesh axis runs over, the one named last changes fastest.
Arguments:
- tokens: bfloat16 [32768, 4096], P(('dp', 'context', 'tensor')), parts along dimension 0, may hold values from -6 to 6
- norm_gain: bfloat16 [4096], replicated, may hold values from 0.099609375 to 1.8984375
- w_query: bfloat16 [4096, 2048], P(None, 'tensor'), may hold values from -2.03125 to 2.03125
- key_matrix: bfloat16 [4096, 1024], P(None, 'tensor'), may hold values from -0.109375 to 0.109375
- value_matrix: bfloat16 [4096, 1024], P(None, 'tensor'), may hold values from -0.09375 to 0.09375
- seg_ids: int32 [32768], P('dp'), parts along dimension 0, may hold values from 0 to 7, never falling along the last dimension, each value on 1 to 4096 neighbouring positions
Outputs:
- attended: bfloat16 [32768, 2048], P(('dp', 'context'), 'tensor'), parts along dimension 0
There are 4 independent parts, one for each index of `dp`. A program takes and returns all parts, laid end to end along the dimension named above; an argument that names none is the same for every part. Nothing has to cross between parts.
Inputs may be any that keep to these rules, and one draw needn't show every extreme that they name: `seg_ids`: never falls along the row; each of the 8 documents covers 1 to 4096 positions, one exactly 4096.
All inputs are finite; a program needn't handle non-finite values.
Results may differ from a plain program's by a relative error of at most 0.0078.
Values may be sent and summed in bfloat16 or wider, within the bound.
A program may use at most 64 MiB of HBM per device.

v0:
```python
import math
import jax
import jax.numpy as jnp
from jax import lax
from jax.sharding import PartitionSpec as P

HEAD_SIZE = 128


def sent_together(arrays, axis, dim, along):
    widths = [a.shape[along] for a in arrays]
    both = jnp.concatenate(arrays, axis=along)
    filled = lax.all_gather(both, axis, axis=dim, tiled=True)
    return tuple(jnp.split(filled, [sum(widths[:k]) for k in range(1, len(widths))], axis=along))


def rotate(vectors, positions):
    half_width = vectors.shape[-1] // 2
    inv_freq = jnp.exp(
        -(jnp.arange(half_width, dtype=jnp.float32) * (2.0 / vectors.shape[-1]))
        * math.log(500000.0)
    )
    angles = positions.astype(jnp.float32)[:, None] * inv_freq[None, :]
    cosine = jnp.cos(angles)[:, None, :]
    sine = jnp.sin(angles)[:, None, :]
    front_half = vectors[..., :half_width]
    back_half = vectors[..., half_width:]
    return jnp.concatenate(
        [front_half * cosine - back_half * sine, back_half * cosine + front_half * sine], -1
    )


def merge_block(
    states_in, query_heads, query_pos, query_segs, key_part, val_part, key_segs, key_pos
):
    peak_old, totals, weighted = states_in
    scores = jnp.einsum(
        "qkgd,skd->kgqs", query_heads, key_part, preferred_element_type=jnp.float32
    ) * (1.0 / math.sqrt(HEAD_SIZE))
    visible = (key_pos[None, :] <= query_pos[:, None]) & (key_segs[None, :] == query_segs[:, None])
    scores = jnp.where(visible[None, None], scores, -1e30)
    peak_new = jnp.maximum(peak_old, jnp.max(scores, -1))
    probs = jnp.where(visible[None, None], jnp.exp(scores - peak_new[..., None]), 0.0)
    rescale = jnp.exp(peak_old - peak_new)
    totals = totals * rescale + jnp.sum(probs, -1)
    weighted = weighted * rescale[..., None] + jnp.einsum(
        "kgqs,skd->kgqd", probs.astype(jnp.bfloat16), val_part, preferred_element_type=jnp.float32
    )
    return (peak_new, totals, weighted)


def body(tokens, norm_gain, w_query, key_matrix, value_matrix, seg_ids):
    wide_tokens = tokens.astype(jnp.float32)
    rms_normalized = (
        wide_tokens
        * lax.rsqrt(jnp.mean(wide_tokens * wide_tokens, -1, keepdims=True) + 1e-05)
        * norm_gain.astype(jnp.float32)
    ).astype(jnp.bfloat16)
    pieces = lax.all_gather(rms_normalized, "tensor", axis=0, tiled=True)
    projected = jnp.concatenate(
        [
            jnp.dot(pieces, w_query, preferred_element_type=jnp.float32),
            jnp.dot(pieces, key_matrix, preferred_element_type=jnp.float32),
            jnp.dot(pieces, value_matrix, preferred_element_type=jnp.float32),
        ],
        1,
    )
    span_rows = projected.shape[0]
    width_q = w_query.shape[1]
    width_k = key_matrix.shape[1]
    heads_q = width_q // HEAD_SIZE
    heads_kv = width_k // HEAD_SIZE
    heads_per_group = heads_q // heads_kv
    offset = lax.axis_index("context") * span_rows
    positions = offset + jnp.arange(span_rows, dtype=jnp.int32)
    query = rotate(projected[:, :width_q].reshape(span_rows, heads_q, HEAD_SIZE), positions).astype(
        jnp.bfloat16
    )
    key = rotate(
        projected[:, width_q : width_q + width_k].reshape(span_rows, heads_kv, HEAD_SIZE), positions
    ).astype(jnp.bfloat16)
    key = key.reshape(span_rows, width_k)
    value_rows = projected[:, width_q + width_k :].astype(jnp.bfloat16)
    groups = (query, positions, lax.dynamic_slice_in_dim(seg_ids, offset, span_rows, 0))
    query_rows, query_pos, query_segs = groups
    count = query_rows.shape[0]
    prepared = [
        (query_rows.reshape(count, heads_kv, heads_per_group, HEAD_SIZE), query_pos, query_segs)
    ]
    initial = [
        (
            jnp.full((heads_kv, heads_per_group, count), -1e30, jnp.float32),
            jnp.zeros((heads_kv, heads_per_group, count), jnp.float32),
            jnp.zeros((heads_kv, heads_per_group, count, HEAD_SIZE), jnp.float32),
        )
    ]
    states = tuple(initial)
    anchor = jnp.int32(0)
    keys_in, values_in = sent_together((key, value_rows), "context", 0, 1)
    length = keys_in.shape[0]
    sub_rows = math.gcd(length, 512)
    parts_count = length // sub_rows
    key_blocks = keys_in.reshape(parts_count, sub_rows, heads_kv, HEAD_SIZE)
    value_blocks = values_in.reshape(parts_count, sub_rows, heads_kv, HEAD_SIZE)
    key_pos_all = jnp.arange(length, dtype=jnp.int32)
    seg_blocks = seg_ids.reshape(parts_count, sub_rows)
    pos_blocks = key_pos_all.reshape(parts_count, sub_rows)
    results = []
    for (query_heads, query_pos, query_segs), states_in in zip(prepared, states):
        skipped = (anchor > jnp.max(query_pos)) | (seg_ids[length - 1] < jnp.min(query_segs))

        def update(carried, query_heads=query_heads, query_pos=query_pos, query_segs=query_segs):

            def inner(running, slices):
                key_part, val_part, key_segs, key_pos = slices
                return (
                    merge_block(
                        running,
                        query_heads,
                        query_pos,
                        query_segs,
                        key_part,
                        val_part,
                        key_segs,
                        key_pos,
                    ),
                    None,
                )

            return lax.scan(inner, carried, (key_blocks, value_blocks, seg_blocks, pos_blocks))[0]

        results.append(lax.cond(skipped, lambda carried: carried, update, states_in))
    finals = tuple(results)
    outputs = []
    for peak_val, totals, weighted in finals:
        count = weighted.shape[2]
        normalized = weighted / totals[..., None]
        outputs.append(
            jnp.transpose(normalized, (2, 0, 1, 3)).reshape(count, width_q).astype(jnp.bfloat16)
        )
    return outputs[0]


def solution(mesh):
    in_specs = (
        P(("dp", "context", "tensor"), None),
        P(),
        P(None, "tensor"),
        P(None, "tensor"),
        P(None, "tensor"),
        P("dp"),
    )
    out_specs = P(("dp", "context"), "tensor")
    return jax.shard_map(body, mesh=mesh, in_specs=in_specs, out_specs=out_specs, check_vma=False)
```

profile of v0, /device:TPU:8, one launch (start us, length us, event | category | flops | bytes accessed | tf_op | source)
XLA Modules:
  0.0 281.3 jit_solution(2508843274565658553)
XLA Ops:
  10.8 60.4 %all-gather.3.cloned.1.call-done = bf16[512,4096]{1,0:T(8,128)(2,1)} async-done(((bf16[64,4096]{1,0:T(8,128)(2,1)}), bf16[512,4096]{1,0:T(8,128)(2,1)}) %all-gather.3.cloned.1.call-update) | async-done | bytes 4194320 | tf_op jit(solution)/shard_map/all_gather | solution.py:59
  71.2 4.1 %convolution_bitcast_fusion.1 = f32[512,1,128]{0,2,1:T(8,128)S(1)} fusion(bf16[512,4096]{1,0:T(8,128)(2,1)} %all-gather.3.cloned.1.call-done, bf16[4096,128]{1,0:T(8,128)(2,1)} %param.13), kind=kOutput, calls=%fused_computation.37 | convolution fusion | flops 536870912 | bytes 5505024 | tf_op jit(solution)/shard_map/dot_general | solution.py:63
  84.1 3.5 %fusion.44 = f32[512,256]{0,1:T(8,128)S(1)} fusion(bf16[512,4096]{1,0:T(8,128)(2,1)} %all-gather.3.cloned.1.call-done, bf16[4096,256]{1,0:T(8,128)(2,1)S(1)} %copy-done), kind=kOutput, calls=%fused_computation.73 | convolution fusion | flops 1073741824 | bytes 6815744 | tf_op jit(solution)/shard_map/dot_general | solution.py:62
  89.4 69.8 %all-gather.5.cloned.1.call-done = bf16[8192,256]{0,1:T(8,128)(2,1)} async-done(((bf16[512,256]{0,1:T(8,128)(2,1)}), bf16[8192,256]{0,1:T(8,128)(2,1)}) %all-gather.5.cloned.1.call-update) | async-done | bytes 4194320 | tf_op jit(solution)/shard_map/all_gather | solution.py:13
  159.2 114.0 %conditional.1 = (f32[1,2,512]{2,1,0:T(2,128)S(1)}, f32[1,2,512,128]{3,2,1,0:T(8,128)S(1)}) conditional(s32[]{:T(128)} %convert_element_type.47, (bf16[8192,256]{0,1:T(8,128)(2,1)}, s32[8192]{0:T(1024)S(1)}, s32[16,512]{1,0:T(8,128)S(1)}, s32[16,512]{1,0:T(8,128)S(1)}, s32[512]{0:T(512)S(1)}, /*index=5*/s32[512]{0:T(512)S(1)}, ...), branch_computations={%region_3.8_spmd, %region_8.9_spmd} | conditional | flops 276453376 | bytes 34325800 | solution.py:132
  159.2 6.4 %copy.10 = bf16[8192,256]{1,0:T(8,128)(2,1)} copy(bf16[8192,256]{0,1:T(8,128)(2,1)} %get-tuple-element.134) | data formatting | bytes 8388608 | tf_op jit(solution)/shard_map
  165.6 4.5 %fusion.42 = (bf16[8192,128]{1,0:T(8,128)(2,1)}, bf16[8192,128]{1,0:T(8,128)(2,1)}) fusion(bf16[8192,256]{1,0:T(8,128)(2,1)} %copy.10), kind=kLoop, calls=%fused_computation.71 | loop fusion | bytes 8388608 | tf_op jit(solution)/shard_map/split | solution.py:14
  170.1 103.1 %while.14 = (s32[]{:T(128)}, f32[1,2,512]{2,1,0:T(2,128)S(1)}, f32[1,2,512]{2,1,0:T(2,128)S(1)}, f32[1,2,512,128]{3,2,1,0:T(8,128)S(1)}, s32[16,512]{1,0:T(8,128...) while((s32[]{:T(128)}, f32[1,2,512]{2,1,0:T(2,128)S(1)}, ...), condition=%wide.region_7.7_spmd.clone, body=%wide.region_4.6_spmd.clone.sunk | while | flops 276436992 | bytes 17384616 | solution.py:130
  170.4 2.8 fusion.59
  176.9 2.8 fusion.59
  183.3 2.8 fusion.59
  189.8 2.8 fusion.59
  196.2 2.8 fusion.59
  202.6 2.8 fusion.59
  209.1 2.8 fusion.59
  215.5 2.8 fusion.59
  222.0 2.8 fusion.59
  228.4 2.8 fusion.59
  234.9 2.8 fusion.59
  241.3 2.8 fusion.59
  247.7 2.8 fusion.59
  254.2 2.8 fusion.59
  260.6 2.8 fusion.59
  267.1 2.8 fusion.59
  (185 shorter events, 71.6 us)
Async XLA Ops:
  6.5 77.6 %copy-start = (bf16[4096,256]{1,0:T(8,128)(2,1)S(1)}, bf16[4096,256]{1,0:T(8,128)(2,1)}, u32[]{:S(2)}) copy-start(bf16[4096,256]{1,0:T(8,128)(2,1)} %param.12) | copy-start | bytes 6291460
  6.5 64.7 %all-gather.3.cloned.1.call-start = ((), (), s32[]{:S(2)}) async-start(), calls=%async_computation | async-start | bytes 4718592 | tf_op jit(solution)/shard_map/all_gather | solution.py:59
  10.7 148.5 %all-gather.5.cloned.1.call-start = ((), (), s32[]{:S(2)}) async-start(), calls=%async_computation.1 | async-start | bytes 4456448 | tf_op jit(solution)/shard_map/all_gather | solution.py:13
  10.8 65.1 %copy-start.3 = (bf16[4096,128]{1,0:T(8,128)(2,1)S(1)}, bf16[4096,128]{1,0:T(8,128)(2,1)}, u32[]{:S(2)}) copy-start(bf16[4096,128]{1,0:T(8,128)(2,1)} %param.14) | copy-start | bytes 3145732
  71.2 4.7 %copy-start.2 = (bf16[512,4096]{1,0:T(8,128)(2,1)S(1)}, bf16[512,4096]{1,0:T(8,128)(2,1)}, u32[]{:S(2)}) copy-start(bf16[512,4096]{1,0:T(8,128)(2,1)} %all-gather.3.cloned.1.call-done) | copy-start | bytes 12582916
  75.9 3.0 %copy-start.4 = (s32[8192]{0:T(1024)S(1)}, s32[8192]{0:T(1024)}, u32[]{:S(2)}) copy-start(s32[8192]{0:T(1024)} %param.15) | copy-start | bytes 98308
  173.2 2.7 copy-start.1
  179.7 2.7 copy-start.1
  186.1 2.7 copy-start.1
  192.6 2.7 copy-start.1
  199.0 2.7 copy-start.1
  205.4 2.7 copy-start.1
  211.9 2.7 copy-start.1
  218.3 2.7 copy-start.1
  224.8 2.7 copy-start.1
  231.2 2.7 copy-start.1
  237.6 2.7 copy-start.1
  244.1 2.7 copy-start.1
  250.5 2.7 copy-start.1
  257.0 2.7 copy-start.1
  263.4 2.7 copy-start.1
  269.9 2.7 copy-start.1
Sparse Core Ops, SparseCore 0:
  10.8 60.3 all-gather.2
  78.3 80.8 all-gather.4
where the time goes:
time: 282 us; the launch traced here: 281 us
  waiting for transfers between devices  130 us (46%)
  matrix products  96.7 us (34%)
  other arithmetic  24.4 us (9%)
  between operations  15.6 us (6%)
  local copies, waits for them, and re-layouts  13.3 us (5%)
    all_gather x1, waiting for transfers between devices, sent_together(): filled = lax.all_gather(both, axis, axis=dim, tiled=True)  69.8 us
    all_gather x1, waiting for transfers between devices, body(): pieces = lax.all_gather(rms_normalized, 'tensor', axis=0, tiled=True)  60.4 us
    dot_general x16, matrix products, merge_block(): jnp.einsum('qkgd,skd->kgqs', query_heads, key_part, preferred_element_typ...  44.4 us
    dot_general x16, matrix products, merge_block(): jnp.einsum('kgqs,skd->kgqd', probs.astype(jnp.bfloat16), val_part, prefer...  43.2 us
    reduce_sum x16, other arithmetic, merge_block(): totals = totals * rescale + jnp.sum(probs, -1)  9.2 us
    another operation x1, local copies, waits for them, and re-layouts  6.43 us
  transfers between devices with their start and end apart: 2, of which 2 were waited for; matrix products, arithmetic and copies ran while one was open for 3% of the time, Pallas kernels for 0%

commit v1 on v0

--- a/solution.py
+++ b/solution.py
@@ -56,7 +56,23 @@
         * lax.rsqrt(jnp.mean(wide_tokens * wide_tokens, -1, keepdims=True) + 1e-05)
         * norm_gain.astype(jnp.float32)
     ).astype(jnp.bfloat16)
-    pieces = lax.all_gather(rms_normalized, "tensor", axis=0, tiled=True)
+    ways, here, turn = (lax.axis_size("tensor"), lax.axis_index("tensor"), rms_normalized.shape[0])
+    dims = [n * ways if d == 0 else n for d, n in enumerate(rms_normalized.shape)]
+    full = lax.dynamic_update_slice_in_dim(
+        jnp.zeros(dims, rms_normalized.dtype), rms_normalized, here * turn, axis=0
+    )
+    going_up = going_down = rms_normalized
+    for far in range(1, ways // 2 + 1):
+        going_up = lax.ppermute(going_up, "tensor", [(d, (d + 1) % ways) for d in range(ways)])
+        full = lax.dynamic_update_slice_in_dim(full, going_up, (here - far) % ways * turn, axis=0)
+        if 2 * far < ways:
+            going_down = lax.ppermute(
+                going_down, "tensor", [(d, (d - 1) % ways) for d in range(ways)]
+            )
+            full = lax.dynamic_update_slice_in_dim(
+                full, going_down, (here + far) % ways * turn, axis=0
+            )
+    pieces = full
     projected = jnp.concatenate(
         [
             jnp.dot(pieces, w_query, preferred_element_type=jnp.float32),

time: 282 us -> 292 us (1.035)
  starting transfers between devices: 0.04 us -> 27.2 us
  waiting for transfers between devices: 130 us -> 104 us
  local copies, waits for them, and re-layouts: 13.3 us -> 21.7 us
    all_gather x1 -> x0, waiting for transfers between devices: 60.4 us -> none  [body(): pieces = lax.all_gather(rms_normalized, 'tensor', axis=0, tiled=True)]
    ppermute x0 -> x7, starting transfers between devices: none -> 27.2 us  [the longest x4 16.2 us: body(): lax.ppermute(going_up, 'tensor', [(d, (d + 1) % ways) for d in range(ways)])]
    ppermute x0 -> x7, waiting for transfers between devices: none -> 24.2 us  [the longest x4 23.2 us: body(): lax.ppermute(going_up, 'tensor', [(d, (d + 1) % ways) for d in range(ways)])]
    all_gather x1, waiting for transfers between devices: 69.8 us -> 79.4 us  [sent_together(): filled = lax.all_gather(both, axis, axis=dim, tiled=True)]
    dynamic_update_slice x0 -> x7, local copies, waits for them, and re-layouts: none -> 5.93 us  [the longest x4 3.38 us: body(): lax.dynamic_update_slice_in_dim(full, going_up, (here - far) % ways * tur...]
  transfers between devices with their start and end apart: 2 -> 8, of which waited for: 2 -> 7; matrix products, arithmetic and copies ran while one was open for 3% -> 5% of each run, Pallas kernels for 0% -> 0%
where the time goes in v1:
time: 292 us; the launch traced here: 291 us
  waiting for transfers between devices  104 us (36%)
  matrix products  98.8 us (34%)
  starting transfers between devices  27.2 us (9%)
  other arithmetic  23.5 us (8%)
  local copies, waits for them, and re-layouts  21.7 us (7%)
  between operations  15.5 us (5%)
    all_gather x1, waiting for transfers between devices, sent_together(): filled = lax.all_gather(both, axis, axis=dim, tiled=True)  79.4 us
    dot_general x16, matrix products, merge_block(): jnp.einsum('qkgd,skd->kgqs', query_heads, key_part, preferred_element_typ...  44.6 us
    dot_general x16, matrix products, merge_block(): jnp.einsum('kgqs,skd->kgqd', probs.astype(jnp.bfloat16), val_part, prefer...  43.3 us
    ppermute x4, waiting for transfers between devices, body(): lax.ppermute(going_up, 'tensor', [(d, (d + 1) % ways) for d in range(ways)])  23.2 us
    ppermute x4, starting transfers between devices, body(): lax.ppermute(going_up, 'tensor', [(d, (d + 1) % ways) for d in range(ways)])  16.2 us
    ppermute x3, starting transfers between devices, body(): lax.ppermute(going_down, 'tensor', [(d, (d - 1) % ways) for d in range(wa...  10.9 us
    reduce_sum x16, other arithmetic, merge_block(): totals = totals * rescale + jnp.sum(probs, -1)  9.2 us
    another operation x1, local copies, waits for them, and re-layouts  6.44 us
  transfers between devices with their start and end apart: 8, of which 7 were waited for; matrix products, arithmetic and copies ran while one was open for 5% of the time, Pallas kernels for 0%

profile of v1, /device:TPU:8, one launch (start us, length us, event | category | flops | bytes accessed | tf_op | source)
XLA Modules:
  0.0 291.4 jit_solution(17106018215552027897)
XLA Ops:
  12.3 3.5 %collective-permute-start = (bf16[64,4096]{1,0:T(8,128)(2,1)}, bf16[64,4096]{1,0:T(8,128)(2,1)S(1)}, u32[]{:S(2)}, u32[]{:S(2)}) collective-permute-start(bf16[64,4096]{1,0:T(8,128)(2,1)} %get-tuple-element.166), channel_id=1, source_target_pairs={{0,1},{1,2},{2,3},{3,4},{4,5},{5,6},{6,7},{7,0},{8,9},{9,10},{10,1... | collective-permute-start | bytes 1572872 | tf_op jit(solution)/shard_map/ppermute | solution.py:66
  15.9 6.1 %collective-permute-start.1 = (bf16[64,4096]{1,0:T(8,128)(2,1)}, bf16[64,4096]{1,0:T(8,128)(2,1)S(1)}, u32[]{:S(2)}, u32[]{:S(2)}) collective-permute-start(bf16[64,4096]{1,0:T(8,128)(2,1)} %get-tuple-element.166), channel_id=1, source_target_pairs={{0,7},{1,0},{2,1},{3,2},{4,3},{5,4},{6,5},{7,6},{8,15},{9,8},{10,9... | collective-permute-start | bytes 1572872 | tf_op jit(solution)/shard_map/ppermute | solution.py:69
  22.1 6.0 %collective-permute-done = bf16[64,4096]{1,0:T(8,128)(2,1)S(1)} collective-permute-done((bf16[64,4096]{1,0:T(8,128)(2,1)}, bf16[64,4096]{1,0:T(8,128)(2,1)S(1)}, u32[]{:S(2)}, u32[]{:S(2)}) %collective-permute-start) | collective-permute-done | bytes 524320 | tf_op jit(solution)/shard_map/ppermute | solution.py:66
  28.1 3.5 %collective-permute-start.2 = (bf16[64,4096]{1,0:T(8,128)(2,1)S(1)}, bf16[64,4096]{1,0:T(8,128)(2,1)S(1)}, u32[]{:S(2)}, u32[]{:S(2)}) collective-permute-start(bf16[64,4096]{1,0:T(8,128)(2,1)S(1)} %collective-permute-done), channel_id=1, source_target_pairs={{0,1},{1,2},{2,3},{3,4},{4,5},{5,6},{6,7},{7,0},{8,9},{9,10},{10,1... | collective-permute-start | bytes 1572872 | tf_op jit(solution)/shard_map/ppermute | solution.py:66
  31.6 2.8 collective-permute-start.3
  36.2 5.8 %collective-permute-done.2 = bf16[64,4096]{1,0:T(8,128)(2,1)S(1)} collective-permute-done((bf16[64,4096]{1,0:T(8,128)(2,1)S(1)}, bf16[64,4096]{1,0:T(8,128)(2,1)S(1)}, u32[]{:S(2)}, u32[]{:S(2)}) %collective-permute-start.2) | collective-permute-done | bytes 524320 | tf_op jit(solution)/shard_map/ppermute | solution.py:66
  42.0 4.3 %collective-permute-start.4 = (bf16[64,4096]{1,0:T(8,128)(2,1)S(1)}, bf16[64,4096]{1,0:T(8,128)(2,1)S(1)}, u32[]{:S(2)}, u32[]{:S(2)}) collective-permute-start(bf16[64,4096]{1,0:T(8,128)(2,1)S(1)} %collective-permute-done.2), channel_id=1, source_target_pairs={{0,1},{1,2},{2,3},{3,4},{4,5},{5,6},{6,7},{7,0},{8,9},{9,10},{10,1... | collective-permute-start | bytes 1572872 | tf_op jit(solution)/shard_map/ppermute | solution.py:66
  50.6 5.1 %collective-permute-done.4 = bf16[64,4096]{1,0:T(8,128)(2,1)S(1)} collective-permute-done((bf16[64,4096]{1,0:T(8,128)(2,1)S(1)}, bf16[64,4096]{1,0:T(8,128)(2,1)S(1)}, u32[]{:S(2)}, u32[]{:S(2)}) %collective-permute-start.4) | collective-permute-done | bytes 524320 | tf_op jit(solution)/shard_map/ppermute | solution.py:66
  55.7 4.9 %collective-permute-start.6 = (bf16[64,4096]{1,0:T(8,128)(2,1)S(1)}, bf16[64,4096]{1,0:T(8,128)(2,1)S(1)}, u32[]{:S(2)}, u32[]{:S(2)}) collective-permute-start(bf16[64,4096]{1,0:T(8,128)(2,1)S(1)} %collective-permute-done.4), channel_id=1, source_target_pairs={{0,1},{1,2},{2,3},{3,4},{4,5},{5,6},{6,7},{7,0},{8,9},{9,10},{10,1... | collective-permute-start | bytes 1572872 | tf_op jit(solution)/shard_map/ppermute | solution.py:66
  62.7 6.4 %collective-permute-done.6 = bf16[64,4096]{1,0:T(8,128)(2,1)S(1)} collective-permute-done((bf16[64,4096]{1,0:T(8,128)(2,1)S(1)}, bf16[64,4096]{1,0:T(8,128)(2,1)S(1)}, u32[]{:S(2)}, u32[]{:S(2)}) %collective-permute-start.6) | collective-permute-done | bytes 524320 | tf_op jit(solution)/shard_map/ppermute | solution.py:66
  69.9 3.8 %convolution_bitcast_fusion.1 = f32[512,1,128]{0,2,1:T(8,128)S(1)} fusion(bf16[512,4096]{1,0:T(8,128)(2,1)} %constant_dynamic-update-slice_fusion, bf16[4096,128]{1,0:T(8,128)(2,1)S(1)} %copy-done.4), kind=kOutput, calls=%fused_computation.37 | convolution fusion | flops 536870912 | bytes 5505024 | tf_op jit(solution)/shard_map/dot_general | solution.py:79
  73.7 3.7 %convolution_convert_fusion = bf16[512,128]{0,1:T(8,128)(2,1)S(1)} fusion(bf16[512,4096]{1,0:T(8,128)(2,1)} %constant_dynamic-update-slice_fusion, bf16[4096,128]{1,0:T(8,128)(2,1)S(1)} %copy-done.3), kind=kOutput, calls=%fused_computation.38 | convolution fusion | flops 536936448 | bytes 5373952 | tf_op jit(solution)/shard_map/dot_general | solution.py:80
  84.4 3.5 %fusion.45 = f32[512,256]{0,1:T(8,128)S(1)} fusion(bf16[512,4096]{1,0:T(8,128)(2,1)} %constant_dynamic-update-slice_fusion, bf16[4096,256]{1,0:T(8,128)(2,1)S(1)} %copy-done), kind=kOutput, calls=%fused_computation.81 | convolution fusion | flops 1073741824 | bytes 6815744 | tf_op jit(solution)/shard_map/dot_general | solution.py:78
  89.6 79.4 %all-gather.2.cloned.1.call-done = bf16[8192,256]{0,1:T(8,128)(2,1)} async-done(((bf16[512,256]{0,1:T(8,128)(2,1)}), bf16[8192,256]{0,1:T(8,128)(2,1)}) %all-gather.2.cloned.1.call-update) | async-done | bytes 4194320 | tf_op jit(solution)/shard_map/all_gather | solution.py:13
  169.0 114.3 %conditional.1 = (f32[1,2,512]{2,1,0:T(2,128)S(1)}, f32[1,2,512,128]{3,2,1,0:T(8,128)S(1)}) conditional(s32[]{:T(128)} %convert_element_type.47, (bf16[8192,256]{0,1:T(8,128)(2,1)}, s32[8192]{0:T(1024)S(1)}, s32[16,512]{1,0:T(8,128)S(1)}, s32[16,512]{1,0:T(8,128)S(1)}, s32[512]{0:T(512)S(1)}, /*index=5*/s32[512]{0:T(512)S(1)}, ...), branch_computations={%region_3.8_spmd, %region_8.9_spmd} | conditional | flops 276453376 | bytes 34325800 | solution.py:148
  169.0 6.4 %copy.10 = bf16[8192,256]{1,0:T(8,128)(2,1)} copy(bf16[8192,256]{0,1:T(8,128)(2,1)} %get-tuple-element.134) | data formatting | bytes 8388608 | tf_op jit(solution)/shard_map
  175.4 4.5 %fusion.43 = (bf16[8192,128]{1,0:T(8,128)(2,1)}, bf16[8192,128]{1,0:T(8,128)(2,1)}) fusion(bf16[8192,256]{1,0:T(8,128)(2,1)} %copy.10), kind=kLoop, calls=%fused_computation.79 | loop fusion | bytes 8388608 | tf_op jit(solution)/shard_map/split | solution.py:14
  179.9 103.3 %while.14 = (s32[]{:T(128)}, f32[1,2,512]{2,1,0:T(2,128)S(1)}, f32[1,2,512]{2,1,0:T(2,128)S(1)}, f32[1,2,512,128]{3,2,1,0:T(8,128)S(1)}, s32[16,512]{1,0:T(8,128...) while((s32[]{:T(128)}, f32[1,2,512]{2,1,0:T(2,128)S(1)}, ...), condition=%wide.region_7.7_spmd.clone, body=%wide.region_4.6_spmd.clone.sunk | while | flops 276436992 | bytes 17384616 | solution.py:146
  180.3 2.8 fusion.60
  193.2 2.8 fusion.60
  212.6 2.8 fusion.60
  225.5 2.8 fusion.60
  244.9 2.8 fusion.60
  264.2 2.8 fusion.60
  (205 shorter events, 108.4 us)
Async XLA Ops:
  6.5 77.8 %copy-start = (bf16[4096,256]{1,0:T(8,128)(2,1)S(1)}, bf16[4096,256]{1,0:T(8,128)(2,1)}, u32[]{:S(2)}) copy-start(bf16[4096,256]{1,0:T(8,128)(2,1)} %param.12) | copy-start | bytes 6291460
  6.5 162.5 %all-gather.2.cloned.1.call-start = ((), (), s32[]{:S(2)}) async-start(), calls=%async_computation | async-start | bytes 4456448 | tf_op jit(solution)/shard_map/all_gather | solution.py:13
  12.3 15.8 %collective-permute-start = (bf16[64,4096]{1,0:T(8,128)(2,1)}, bf16[64,4096]{1,0:T(8,128)(2,1)S(1)}, u32[]{:S(2)}, u32[]{:S(2)}) collective-permute-start(bf16[64,4096]{1,0:T(8,128)(2,1)} %get-tuple-element.166), channel_id=1, source_target_pairs={{0,1},{1,2},{2,3},{3,4},{4,5},{5,6},{6,7},{7,0},{8,9},{9,10},{10,1... | collective-permute-start | bytes 1572872 | tf_op jit(solution)/shard_map/ppermute | solution.py:66
  15.9 15.8 %collective-permute-start.1 = (bf16[64,4096]{1,0:T(8,128)(2,1)}, bf16[64,4096]{1,0:T(8,128)(2,1)S(1)}, u32[]{:S(2)}, u32[]{:S(2)}) collective-permute-start(bf16[64,4096]{1,0:T(8,128)(2,1)} %get-tuple-element.166), channel_id=1, source_target_pairs={{0,7},{1,0},{2,1},{3,2},{4,3},{5,4},{6,5},{7,6},{8,15},{9,8},{10,9... | collective-permute-start | bytes 1572872 | tf_op jit(solution)/shard_map/ppermute | solution.py:69
  28.1 13.9 %collective-permute-start.2 = (bf16[64,4096]{1,0:T(8,128)(2,1)S(1)}, bf16[64,4096]{1,0:T(8,128)(2,1)S(1)}, u32[]{:S(2)}, u32[]{:S(2)}) collective-permute-start(bf16[64,4096]{1,0:T(8,128)(2,1)S(1)} %collective-permute-done), channel_id=1, source_target_pairs={{0,1},{1,2},{2,3},{3,4},{4,5},{5,6},{6,7},{7,0},{8,9},{9,10},{10,1... | collective-permute-start | bytes 1572872 | tf_op jit(solution)/shard_map/ppermute | solution.py:66
  31.6 15.2 %collective-permute-start.3 = (bf16[64,4096]{1,0:T(8,128)(2,1)S(1)}, bf16[64,4096]{1,0:T(8,128)(2,1)S(1)}, u32[]{:S(2)}, u32[]{:S(2)}) collective-permute-start(bf16[64,4096]{1,0:T(8,128)(2,1)S(1)} %collective-permute-done.1), channel_id=1, source_target_pairs={{0,7},{1,0},{2,1},{3,2},{4,3},{5,4},{6,5},{7,6},{8,15},{9,8},{10,9... | collective-permute-start | bytes 1572872 | tf_op jit(solution)/shard_map/ppermute | solution.py:69
  42.0 13.6 %collective-permute-start.4 = (bf16[64,4096]{1,0:T(8,128)(2,1)S(1)}, bf16[64,4096]{1,0:T(8,128)(2,1)S(1)}, u32[]{:S(2)}, u32[]{:S(2)}) collective-permute-start(bf16[64,4096]{1,0:T(8,128)(2,1)S(1)} %collective-permute-done.2), channel_id=1, source_target_pairs={{0,1},{1,2},{2,3},{3,4},{4,5},{5,6},{6,7},{7,0},{8,9},{9,10},{10,1... | collective-permute-start | bytes 1572872 | tf_op jit(solution)/shard_map/ppermute | solution.py:66
  46.9 15.0 %collective-permute-start.5 = (bf16[64,4096]{1,0:T(8,128)(2,1)S(1)}, bf16[64,4096]{1,0:T(8,128)(2,1)S(1)}, u32[]{:S(2)}, u32[]{:S(2)}) collective-permute-start(bf16[64,4096]{1,0:T(8,128)(2,1)S(1)} %collective-permute-done.3), channel_id=1, source_target_pairs={{0,7},{1,0},{2,1},{3,2},{4,3},{5,4},{6,5},{7,6},{8,15},{9,8},{10,9... | collective-permute-start | bytes 1572872 | tf_op jit(solution)/shard_map/ppermute | solution.py:69
  49.7 20.2 %copy-start.4 = (bf16[4096,128]{1,0:T(8,128)(2,1)S(1)}, bf16[4096,128]{1,0:T(8,128)(2,1)}, u32[]{:S(2)}) copy-start(bf16[4096,128]{1,0:T(8,128)(2,1)} %param.13) | copy-start | bytes 3145732
  55.7 13.4 %collective-permute-start.6 = (bf16[64,4096]{1,0:T(8,128)(2,1)S(1)}, bf16[64,4096]{1,0:T(8,128)(2,1)S(1)}, u32[]{:S(2)}, u32[]{:S(2)}) collective-permute-start(bf16[64,4096]{1,0:T(8,128)(2,1)S(1)} %collective-permute-done.4), channel_id=1, source_target_pairs={{0,1},{1,2},{2,3},{3,4},{4,5},{5,6},{6,7},{7,0},{8,9},{9,10},{10,1... | collective-permute-start | bytes 1572872 | tf_op jit(solution)/shard_map/ppermute | solution.py:66
  69.9 3.8 %copy-start.3 = (bf16[4096,128]{1,0:T(8,128)(2,1)S(1)}, bf16[4096,128]{1,0:T(8,128)(2,1)}, u32[]{:S(2)}) copy-start(bf16[4096,128]{1,0:T(8,128)(2,1)} %param.14) | copy-start | bytes 3145732
  73.7 5.7 %copy-start.5 = (s32[8192]{0:T(1024)S(1)}, s32[8192]{0:T(1024)}, u32[]{:S(2)}) copy-start(s32[8192]{0:T(1024)} %param.15) | copy-start | bytes 98308
  189.5 2.7 copy-start.1
  196.0 2.7 copy-start.1
  202.4 2.7 copy-start.1
  208.9 2.7 copy-start.1
  215.4 2.7 copy-start.1
  221.8 2.7 copy-start.1
  228.3 2.7 copy-start.1
  234.7 2.7 copy-start.1
  241.2 2.7 copy-start.1
  247.7 2.7 copy-start.1
  254.1 2.7 copy-start.1
  260.6 2.7 copy-start.1
  (5 other events, 13.4 us)
Sparse Core Ops, SparseCore 0:
  78.8 90.1 all-gather.1
